TPU v7x, 128 devices: a whole 4x4x4 slice. The times are simulated.
128 devices in a mesh: seq: 32 (over x, y, core), tp: 4 (over z).
Axes of the slice: x: 4, y: 4, z: 4, core: 2. Of those that a mesh axis runs over, the one named last changes fastest.
Arguments:
- states_in: bfloat16 [8192, 2048], P('seq'), may hold values from -7 to 7
- lengths: int32 [4], replicated, may hold values from 1 to 64, 128 in all
- attn_gain: float32 [2048], replicated, may hold values from 0.5 to 1.5
- w_query: bfloat16 [2048, 2048], P(None, 'tp'), may hold values from -0.125 to 0.125
- w_key: bfloat16 [2048, 2048], P(None, 'tp'), may hold values from -0.088388348 to 0.088388348
- w_value: bfloat16 [2048, 4096], P(None, 'tp'), may hold values from -0.125 to 0.125
- w_gate: bfloat16 [2048, 4096], P(None, 'tp'), may hold values from -0.125 to 0.125
- w_beta: bfloat16 [2048, 16], P(None, 'tp'), may hold values from -1 to 1
- w_alpha: bfloat16 [2048, 16], P(None, 'tp'), may hold values from -0.125 to 0.125
- decay_rate: float32 [16], P('tp'), may hold values from 4.8828125e-05 to 0.05
- decay_bias: float32 [16], P('tp'), may hold values from -2 to 1
- conv_query: float32 [4, 2048], P(None, 'tp'), may hold values from -3 to 3
- conv_key: float32 [4, 2048], P(None, 'tp'), may hold values from -3 to 3
- conv_value: float32 [4, 4096], P(None, 'tp'), may hold values from -4.5 to 4.5
- out_gain: float32 [256], replicated, may hold values from 0.5 to 1.5
- w_out: bfloat16 [4096, 2048], P('tp'), may hold values from -0.09375 to 0.09375
- final_gain: float32 [2048], replicated, may hold values from 0.5 to 1.5
- w_head: bfloat16 [2048, 32000], P(None, ('seq', 'tp')), may hold values from -0.41992188 to 0.41992188
Outputs:
- hidden: bfloat16 [8192, 2048], P('seq', 'tp')
- block_states: float32 [128, 16, 128, 256], P('seq', 'tp')
- max_logit: float32 [4], replicated
Inputs may be any that keep to these rules, and one draw needn't show every extreme that they name: Prompt lengths are counted in blocks of 64 tokens; they sum to 128 and the longest is 64.
All inputs are finite; a program needn't handle non-finite values.
Results may differ from a plain program's by a relative error of at most 0.0095.
Values may be sent and summed in bfloat16 or wider, within the bound.
No kernel may reach another device: no remote copies, remote signals or barrier semaphores. Data moves between devices by JAX's collectives and lax.ppermute only.
A program may use at most 128 MiB of HBM per device.

v0:
```python
import jax
import jax.numpy as jnp
from jax import lax
from jax.sharding import PartitionSpec as P

CONV = 4
BLOCK_LEN = 64
EPS = 1e-06
HIGH = lax.Precision.HIGHEST


def from_behind(value, axis, steps):
    count = lax.axis_size(axis)
    first, last = (max(0, -steps), min(count, count - steps))
    return lax.ppermute(value, axis, [(source, source + steps) for source in range(first, last)])


def rms_scale(values, gain):
    return values * lax.rsqrt(jnp.mean(values * values, axis=-1, keepdims=True) + EPS) * gain


def unit_rows(values):
    return values * lax.rsqrt(jnp.sum(values * values, axis=-1, keepdims=True) + EPS)


def request_start(positions, offsets, block_len):
    block_ids = positions // block_len
    hits = offsets[None, :] <= block_ids[:, None]
    return block_len * jnp.max(jnp.where(hits, offsets[None, :], 0), axis=1)


def short_conv(extended, positions, start_tok, weight):
    row_count = positions.shape[0]
    tap_count = weight.shape[0]
    running = jnp.zeros((row_count, extended.shape[1]), jnp.float32)
    for tap_index in range(tap_count):
        lag_steps = tap_count - 1 - tap_index
        shifted = extended[tap_index : tap_index + row_count].astype(jnp.float32)
        valid = (positions - lag_steps >= start_tok)[:, None]
        running = running + jnp.where(valid, shifted, 0.0) * weight[tap_index]
    return jax.nn.silu(running)


def block_step(carry_state, block_inputs):
    q_rows, k_rows, v_rows, beta_rows, log_cum, keep_flag = block_inputs
    carry_state = carry_state * keep_flag
    block_len = q_rows.shape[1]
    row_ids = lax.broadcasted_iota(jnp.int32, (block_len, block_len), 0)
    col_ids = lax.broadcasted_iota(jnp.int32, (block_len, block_len), 1)
    on_lower = (row_ids >= col_ids).astype(jnp.float32)
    off_lower = (row_ids > col_ids).astype(jnp.float32)
    log_gap = log_cum[:, :, None] - log_cum[:, None, :]
    decays = jnp.exp(jnp.where(row_ids >= col_ids, log_gap, 0.0)) * on_lower
    growth = jnp.exp(log_cum)
    key_gram = jnp.einsum("hid,hjd->hij", k_rows, k_rows, precision=HIGH)
    system_mat = (
        jnp.eye(block_len, dtype=jnp.float32)
        + beta_rows[:, :, None] * key_gram * decays * off_lower
    )
    carried = jnp.einsum("hid,hde->hie", k_rows, carry_state, precision=HIGH)
    right_side = beta_rows[:, :, None] * (v_rows - growth[:, :, None] * carried)
    pseudo_values = lax.linalg.triangular_solve(
        system_mat, right_side, left_side=True, lower=True, unit_diagonal=True
    )
    scores = jnp.einsum("hid,hjd->hij", q_rows, k_rows, precision=HIGH) * decays
    output = growth[:, :, None] * jnp.einsum("hid,hde->hie", q_rows, carry_state, precision=HIGH)
    output = output + jnp.einsum("hij,hje->hie", scores, pseudo_values, precision=HIGH)
    tail_decay = jnp.exp(log_cum[:, -1:] - log_cum)
    carry_state = jnp.exp(log_cum[:, -1])[:, None, None] * carry_state + jnp.einsum(
        "hjd,hje->hde", k_rows * tail_decay[:, :, None], pseudo_values, precision=HIGH
    )
    return (carry_state, (output, carry_state))


def to_blocks(values, block_count, head_count):
    return values.reshape(block_count, BLOCK_LEN, head_count, -1).transpose(0, 2, 1, 3)


def body(
    states_in,
    lengths,
    attn_gain,
    w_query,
    w_key,
    w_value,
    w_gate,
    w_beta,
    w_alpha,
    decay_rate,
    decay_bias,
    conv_query,
    conv_key,
    conv_value,
    out_gain,
    w_out,
    final_gain,
    w_head,
):
    tok_dev = states_in.shape[0]
    heads_dev = decay_rate.shape[0]
    key_dim = w_query.shape[1] // heads_dev
    value_dim = w_value.shape[1] // heads_dev
    blocks_dev = tok_dev // BLOCK_LEN
    piece_index = lax.axis_index("seq")
    x_float = states_in.astype(jnp.float32)
    normed = rms_scale(x_float, attn_gain).astype(jnp.bfloat16)
    pre_q = jnp.dot(normed, w_query, preferred_element_type=jnp.float32).astype(jnp.bfloat16)
    pre_k = jnp.dot(normed, w_key, preferred_element_type=jnp.float32).astype(jnp.bfloat16)
    pre_v = jnp.dot(normed, w_value, preferred_element_type=jnp.float32).astype(jnp.bfloat16)
    gate_raw = jnp.dot(normed, w_gate, preferred_element_type=jnp.float32)
    beta_all = jax.nn.sigmoid(jnp.dot(normed, w_beta, preferred_element_type=jnp.float32))
    log_decay = -decay_rate * jax.nn.softplus(
        jnp.dot(normed, w_alpha, preferred_element_type=jnp.float32) + decay_bias
    )
    ends = jnp.cumsum(lengths)
    offsets = ends - lengths
    positions = piece_index * tok_dev + jnp.arange(tok_dev, dtype=jnp.int32)
    start_tok = request_start(positions, offsets, BLOCK_LEN)
    local_pre = jnp.concatenate([pre_q, pre_k, pre_v], axis=1)
    prev_edge = from_behind(local_pre[tok_dev - (CONV - 1) :], "seq", 1)
    extended = jnp.concatenate([prev_edge, local_pre], axis=0)
    conv_weights = jnp.concatenate([conv_query, conv_key, conv_value], axis=1)
    conv_all = short_conv(extended, positions, start_tok, conv_weights)
    qk_width = heads_dev * key_dim
    q_heads = unit_rows(conv_all[:, :qk_width].reshape(tok_dev, heads_dev, key_dim)) * key_dim ** (
        -0.5
    )
    k_heads = unit_rows(conv_all[:, qk_width : 2 * qk_width].reshape(tok_dev, heads_dev, key_dim))
    q_blocks = to_blocks(q_heads, blocks_dev, heads_dev)
    k_blocks = to_blocks(k_heads, blocks_dev, heads_dev)
    v_blocks = to_blocks(conv_all[:, 2 * qk_width :], blocks_dev, heads_dev)
    v_augmented = jnp.concatenate(
        [jnp.zeros(v_blocks.shape[:3] + (key_dim,), jnp.float32), v_blocks], axis=3
    )
    beta_blocks = beta_all.reshape(blocks_dev, BLOCK_LEN, heads_dev).transpose(0, 2, 1)
    log_blocks = jnp.cumsum(
        log_decay.reshape(blocks_dev, BLOCK_LEN, heads_dev).transpose(0, 2, 1), axis=2
    )
    block_ids = piece_index * blocks_dev + jnp.arange(blocks_dev, dtype=jnp.int32)
    keep_flags = 1.0 - jnp.max((offsets[None, :] == block_ids[:, None]).astype(jnp.float32), axis=1)
    eye_heads = jnp.broadcast_to(jnp.eye(key_dim, dtype=jnp.float32), (heads_dev, key_dim, key_dim))
    initial = jnp.concatenate(
        [eye_heads, jnp.zeros((heads_dev, key_dim, value_dim), jnp.float32)], axis=2
    )
    final_aug, (out_aug, states_aug) = lax.scan(
        block_step, initial, (q_blocks, k_blocks, v_augmented, beta_blocks, log_blocks, keep_flags)
    )
    lin_map = final_aug[:, :, :key_dim]
    offset_state = final_aug[:, :, key_dim:]

    def relay_turn(turn_index, incoming):
        outgoing = jnp.einsum("hde,hef->hdf", lin_map, incoming, precision=HIGH) + offset_state
        return from_behind(outgoing, "seq", 1)

    incoming = lax.fori_loop(0, lax.axis_size("seq") - 1, relay_turn, jnp.zeros_like(offset_state))
    o_blocks = out_aug[..., key_dim:] + jnp.einsum(
        "bhcd,hde->bhce", out_aug[..., :key_dim], incoming, precision=HIGH
    )
    block_states = (
        jnp.einsum("bhde,hef->bhdf", states_aug[..., :key_dim], incoming, precision=HIGH)
        + states_aug[..., key_dim:]
    )
    o_tokens = o_blocks.transpose(0, 2, 1, 3).reshape(tok_dev, heads_dev, value_dim)
    gated = (
        rms_scale(o_tokens, out_gain) * jax.nn.silu(gate_raw.reshape(tok_dev, heads_dev, value_dim))
    ).astype(jnp.bfloat16)
    partial_out = jnp.dot(
        gated.reshape(tok_dev, heads_dev * value_dim), w_out, preferred_element_type=jnp.float32
    )
    model_width = x_float.shape[1]
    share_cols = model_width // lax.axis_size("tp")
    col_start = lax.axis_index("tp") * share_cols
    last_tok = ends * BLOCK_LEN - 1
    picker = (last_tok[:, None] == positions[None, :]).astype(jnp.bfloat16)
    summed = lax.psum(partial_out, "tp")
    hidden_full = (x_float + summed).astype(jnp.bfloat16)
    hidden = lax.dynamic_slice_in_dim(hidden_full, col_start, share_cols, 1)
    picked = jnp.dot(picker, hidden_full, preferred_element_type=jnp.float32)
    last_rows = lax.psum(picked.astype(jnp.bfloat16), "seq").astype(jnp.float32)
    final = rms_scale(last_rows, final_gain).astype(jnp.bfloat16)
    logits = jnp.dot(final, w_head, preferred_element_type=jnp.float32)
    max_logit = lax.pmax(jnp.max(logits, axis=1), ("seq", "tp"))
    return (hidden, block_states, max_logit)


def solution(mesh):
    return jax.shard_map(
        body,
        mesh=mesh,
        in_specs=(
            P("seq", None),
            P(),
            P(),
            P(None, "tp"),
            P(None, "tp"),
            P(None, "tp"),
            P(None, "tp"),
            P(None, "tp"),
            P(None, "tp"),
            P("tp"),
            P("tp"),
            P(None, "tp"),
            P(None, "tp"),
            P(None, "tp"),
            P(),
            P("tp", None),
            P(),
            P(None, ("seq", "tp")),
        ),
        out_specs=(P("seq", "tp"), P("seq", "tp", None, None), P()),
        check_vma=False,
    )
```

profile of v0, /device:TPU:1, one launch (start us, length us, event | category | flops | bytes accessed | tf_op | source)
XLA Modules:
  0.0 931.8 jit_solution(14299696759197903953)
XLA Ops:
  51.5 133.2 %while.24 = (s32[]{:T(128)}, f32[4,128,384]{2,1,0:T(8,128)S(1)}, f32[4,4,64,384]{3,2,0,1:T(8,128)}, f32[4,4,128,384]{3,2,1,0:T(8,128)}, f32[4,4,64]{2,1,0:T(4,12...) while((s32[]{:T(128)}, f32[4,128,384]{2,1,0:T(8,128)S(1)}, ...), condition=%wide.region_8.9_spmd, body=%wide.region_7.8_spmd.sunk | while | flops 656073024 | bytes 11045709 | solution.py:145
  54.5 20.4 %custom-call.8 = f32[4,1,64,64]{2,3,1,0:T(8,128)S(1)} custom-call(f32[4,1,64,64]{3,2,1,0:T(8,128)} %fusion.136), custom_call_target="InvertDiagBlocksLowerTriangular" | custom-call | tf_op jit(solution)/shard_map/while/body/eval_jaxpr/triangular_solve | solution.py:62
  87.8 20.4 %custom-call.8 = f32[4,1,64,64]{2,3,1,0:T(8,128)S(1)} custom-call(f32[4,1,64,64]{3,2,1,0:T(8,128)} %fusion.136), custom_call_target="InvertDiagBlocksLowerTriangular" | custom-call | tf_op jit(solution)/shard_map/while/body/eval_jaxpr/triangular_solve | solution.py:62
  121.1 20.4 %custom-call.8 = f32[4,1,64,64]{2,3,1,0:T(8,128)S(1)} custom-call(f32[4,1,64,64]{3,2,1,0:T(8,128)} %fusion.136), custom_call_target="InvertDiagBlocksLowerTriangular" | custom-call | tf_op jit(solution)/shard_map/while/body/eval_jaxpr/triangular_solve | solution.py:62
  154.4 20.4 %custom-call.8 = f32[4,1,64,64]{2,3,1,0:T(8,128)S(1)} custom-call(f32[4,1,64,64]{3,2,1,0:T(8,128)} %fusion.136), custom_call_target="InvertDiagBlocksLowerTriangular" | custom-call | tf_op jit(solution)/shard_map/while/body/eval_jaxpr/triangular_solve | solution.py:62
  185.6 428.0 %while.25 = (s32[]{:T(128)}, f32[4,128,256]{2,1,0:T(8,128)S(1)}, f32[4,128,128]{2,1,0:T(8,128)}, f32[4,128,256]{2,1,0:T(8,128)S(1)}, s32[]{:T(128)}) while((s32[]{:T(128)}, f32[4,128,256]{2,1,0:T(8,128)S(1)}, f32[4,128,128]{2,1,0:T(8,128)}, f32[4,128,256]{2,1,0:T(8,128)S(1)}, s32[]{:T(128)}) %tuple.75), condition=%wide.region_10.11_spmd, body=%wide.region_9.10_spmd.sunk | while | flops 201457664 | bytes 3932261 | solution.py:155
  189.9 6.4 collective-permute-done
  202.9 6.4 collective-permute-done
  215.9 6.4 collective-permute-done
  228.9 6.4 collective-permute-done
  241.9 6.4 collective-permute-done
  255.0 6.4 collective-permute-done
  268.0 6.4 collective-permute-done
  281.0 6.4 collective-permute-done
  294.0 6.4 collective-permute-done
  307.1 6.4 collective-permute-done
  320.1 6.4 collective-permute-done
  333.1 6.4 collective-permute-done
  346.1 6.4 collective-permute-done
  359.2 6.4 collective-permute-done
  372.2 6.4 collective-permute-done
  385.2 6.4 collective-permute-done
  398.2 6.4 collective-permute-done
  411.3 6.4 collective-permute-done
  425.6 6.4 collective-permute-done
  440.7 6.4 collective-permute-done
  449.5 6.4 collective-permute-start
  455.9 6.4 collective-permute-done
  471.0 6.4 collective-permute-done
  479.7 6.4 collective-permute-start
  486.1 6.4 collective-permute-done
  494.9 6.4 collective-permute-start
  501.3 6.4 collective-permute-done
  516.4 6.4 collective-permute-done
  525.1 6.4 collective-permute-start
  531.5 6.4 collective-permute-done
  546.7 6.4 collective-permute-done
  555.4 6.4 collective-permute-start
  561.8 6.4 collective-permute-done
  570.5 6.4 collective-permute-start
  576.9 6.4 collective-permute-done
  585.7 6.4 collective-permute-start
  592.1 6.4 collective-permute-done
  607.2 6.4 collective-permute-done
  620.6 8.3 fusion.47
  637.6 89.2 %all-reduce.4.cloned.1.call-done = f32[256,2048]{1,0:T(8,128)} async-done(((f32[256,2048]{1,0:T(8,128)}), f32[256,2048]{1,0:T(8,128)}) %all-reduce.4.cloned.1.call-update) | async-done | bytes 2097168 | tf_op jit(solution)/shard_map/psum | solution.py:175
  729.2 123.1 %psum.15 = bf16[4,2048]{1,0:T(4,128)(2,1)S(1)} all-reduce(bf16[4,2048]{1,0:T(4,128)(2,1)S(1)} %convolution_convert_fusion), channel_id=1, replica_groups=mesh['seq'=32,'tp'=4] {'seq'}, use_global_device_ids=true, to_apply=%region_13.14 | all-reduce | flops 8192 | bytes 32768 | tf_op jit(solution)/shard_map/psum | solution.py:179
  857.0 67.2 %pmax.7 = f32[4]{0:T(128)} all-reduce(f32[4]{0:T(128)S(1)} %convolution_reduce_fusion), channel_id=1, replica_groups=mesh['seq'=32,'tp'=4] {'seq','tp'}, use_global_device_ids=true, to_apply=%region_16.17 | all-reduce | flops 4 | bytes 32 | tf_op jit(solution)/shard_map/pmax | solution.py:182
  (279 shorter events, 303.6 us)
Async XLA Ops:
  7.2 5.7 copy-start
  7.2 719.6 %all-reduce.4.cloned.1.call-start = ((), (), s32[]{:S(2)}) async-start(), calls=%async_computation | async-start | bytes 4194304 | tf_op jit(solution)/shard_map/psum | solution.py:175
  8.9 15.2 %copy-start.18 = (f32[256]{0:T(256)}, f32[256]{0:T(256)S(1)}, u32[]{:S(2)}) copy-start(f32[256]{0:T(256)S(1)} %add_rsqrt_fusion.3) | copy-start | bytes 3076
  15.2 5.5 copy-start.20
  15.2 6.3 copy-start.13
  15.3 6.3 copy-start.14
  15.3 6.3 copy-start.11
  15.3 7.1 copy-start.26
  15.3 7.1 copy-start.22
  15.3 8.7 copy-start.17
  15.3 8.8 copy-start.23
  15.3 8.8 copy-start.27
  15.9 12.0 %collective-permute-start.1 = (bf16[3,2048]{1,0:T(4,128)(2,1)S(1)}, bf16[3,2048]{1,0:T(4,128)(2,1)S(1)}, u32[]{:S(2)}, u32[]{:S(2)}) collective-permute-start(bf16[3,2048]{1,0:T(4,128)(2,1)S(1)} %slice.76), channel_id=1, source_target_pairs={{0,4},{4,8},{8,12},{12,16},{16,20},{20,24},{24,28},{28,32},{32,36}... | collective-permute-start | bytes 36872 | tf_op jit(solution)/shard_map/ppermute | solution.py:15
  145.7 4.3 copy-start.6
  179.0 4.3 copy-start.6
  187.9 8.3 collective-permute-start
  198.6 10.7 %collective-permute-start = (f32[4,128,256]{2,1,0:T(8,128)}, f32[4,128,256]{2,1,0:T(8,128)S(1)}, u32[]{:S(2)}, u32[]{:S(2)}) collective-permute-start(f32[4,128,256]{2,1,0:T(8,128)} %convolution_add_fusion.5), channel_id=1, source_target_pairs={{0,4},{4,8},{8,12},{12,16},{16,20},{20,24},{24,28},{28,32},{32,36}... | collective-permute-start | bytes 1572872 | tf_op jit(solution)/shard_map/while/body/eval_jaxpr/ppermute | solution.py:15
  211.6 10.7 %collective-permute-start = (f32[4,128,256]{2,1,0:T(8,128)}, f32[4,128,256]{2,1,0:T(8,128)S(1)}, u32[]{:S(2)}, u32[]{:S(2)}) collective-permute-start(f32[4,128,256]{2,1,0:T(8,128)} %convolution_add_fusion.5), channel_id=1, source_target_pairs={{0,4},{4,8},{8,12},{12,16},{16,20},{20,24},{24,28},{28,32},{32,36}... | collective-permute-start | bytes 1572872 | tf_op jit(solution)/shard_map/while/body/eval_jaxpr/ppermute | solution.py:15
  224.6 10.7 %collective-permute-start = (f32[4,128,256]{2,1,0:T(8,128)}, f32[4,128,256]{2,1,0:T(8,128)S(1)}, u32[]{:S(2)}, u32[]{:S(2)}) collective-permute-start(f32[4,128,256]{2,1,0:T(8,128)} %convolution_add_fusion.5), channel_id=1, source_target_pairs={{0,4},{4,8},{8,12},{12,16},{16,20},{20,24},{24,28},{28,32},{32,36}... | collective-permute-start | bytes 1572872 | tf_op jit(solution)/shard_map/while/body/eval_jaxpr/ppermute | solution.py:15
  237.7 10.7 %collective-permute-start = (f32[4,128,256]{2,1,0:T(8,128)}, f32[4,128,256]{2,1,0:T(8,128)S(1)}, u32[]{:S(2)}, u32[]{:S(2)}) collective-permute-start(f32[4,128,256]{2,1,0:T(8,128)} %convolution_add_fusion.5), channel_id=1, source_target_pairs={{0,4},{4,8},{8,12},{12,16},{16,20},{20,24},{24,28},{28,32},{32,36}... | collective-permute-start | bytes 1572872 | tf_op jit(solution)/shard_map/while/body/eval_jaxpr/ppermute | solution.py:15
  250.7 10.7 %collective-permute-start = (f32[4,128,256]{2,1,0:T(8,128)}, f32[4,128,256]{2,1,0:T(8,128)S(1)}, u32[]{:S(2)}, u32[]{:S(2)}) collective-permute-start(f32[4,128,256]{2,1,0:T(8,128)} %convolution_add_fusion.5), channel_id=1, source_target_pairs={{0,4},{4,8},{8,12},{12,16},{16,20},{20,24},{24,28},{28,32},{32,36}... | collective-permute-start | bytes 1572872 | tf_op jit(solution)/shard_map/while/body/eval_jaxpr/ppermute | solution.py:15
  263.7 10.7 %collective-permute-start = (f32[4,128,256]{2,1,0:T(8,128)}, f32[4,128,256]{2,1,0:T(8,128)S(1)}, u32[]{:S(2)}, u32[]{:S(2)}) collective-permute-start(f32[4,128,256]{2,1,0:T(8,128)} %convolution_add_fusion.5), channel_id=1, source_target_pairs={{0,4},{4,8},{8,12},{12,16},{16,20},{20,24},{24,28},{28,32},{32,36}... | collective-permute-start | bytes 1572872 | tf_op jit(solution)/shard_map/while/body/eval_jaxpr/ppermute | solution.py:15
  276.7 10.7 %collective-permute-start = (f32[4,128,256]{2,1,0:T(8,128)}, f32[4,128,256]{2,1,0:T(8,128)S(1)}, u32[]{:S(2)}, u32[]{:S(2)}) collective-permute-start(f32[4,128,256]{2,1,0:T(8,128)} %convolution_add_fusion.5), channel_id=1, source_target_pairs={{0,4},{4,8},{8,12},{12,16},{16,20},{20,24},{24,28},{28,32},{32,36}... | collective-permute-start | bytes 1572872 | tf_op jit(solution)/shard_map/while/body/eval_jaxpr/ppermute | solution.py:15
  289.8 10.7 %collective-permute-start = (f32[4,128,256]{2,1,0:T(8,128)}, f32[4,128,256]{2,1,0:T(8,128)S(1)}, u32[]{:S(2)}, u32[]{:S(2)}) collective-permute-start(f32[4,128,256]{2,1,0:T(8,128)} %convolution_add_fusion.5), channel_id=1, source_target_pairs={{0,4},{4,8},{8,12},{12,16},{16,20},{20,24},{24,28},{28,32},{32,36}... | collective-permute-start | bytes 1572872 | tf_op jit(solution)/shard_map/while/body/eval_jaxpr/ppermute | solution.py:15
  302.8 10.7 %collective-permute-start = (f32[4,128,256]{2,1,0:T(8,128)}, f32[4,128,256]{2,1,0:T(8,128)S(1)}, u32[]{:S(2)}, u32[]{:S(2)}) collective-permute-start(f32[4,128,256]{2,1,0:T(8,128)} %convolution_add_fusion.5), channel_id=1, source_target_pairs={{0,4},{4,8},{8,12},{12,16},{16,20},{20,24},{24,28},{28,32},{32,36}... | collective-permute-start | bytes 1572872 | tf_op jit(solution)/shard_map/while/body/eval_jaxpr/ppermute | solution.py:15
  315.8 10.7 %collective-permute-start = (f32[4,128,256]{2,1,0:T(8,128)}, f32[4,128,256]{2,1,0:T(8,128)S(1)}, u32[]{:S(2)}, u32[]{:S(2)}) collective-permute-start(f32[4,128,256]{2,1,0:T(8,128)} %convolution_add_fusion.5), channel_id=1, source_target_pairs={{0,4},{4,8},{8,12},{12,16},{16,20},{20,24},{24,28},{28,32},{32,36}... | collective-permute-start | bytes 1572872 | tf_op jit(solution)/shard_map/while/body/eval_jaxpr/ppermute | solution.py:15
  328.8 10.7 %collective-permute-start = (f32[4,128,256]{2,1,0:T(8,128)}, f32[4,128,256]{2,1,0:T(8,128)S(1)}, u32[]{:S(2)}, u32[]{:S(2)}) collective-permute-start(f32[4,128,256]{2,1,0:T(8,128)} %convolution_add_fusion.5), channel_id=1, source_target_pairs={{0,4},{4,8},{8,12},{12,16},{16,20},{20,24},{24,28},{28,32},{32,36}... | collective-permute-start | bytes 1572872 | tf_op jit(solution)/shard_map/while/body/eval_jaxpr/ppermute | solution.py:15
  341.9 10.7 %collective-permute-start = (f32[4,128,256]{2,1,0:T(8,128)}, f32[4,128,256]{2,1,0:T(8,128)S(1)}, u32[]{:S(2)}, u32[]{:S(2)}) collective-permute-start(f32[4,128,256]{2,1,0:T(8,128)} %convolution_add_fusion.5), channel_id=1, source_target_pairs={{0,4},{4,8},{8,12},{12,16},{16,20},{20,24},{24,28},{28,32},{32,36}... | collective-permute-start | bytes 1572872 | tf_op jit(solution)/shard_map/while/body/eval_jaxpr/ppermute | solution.py:15
  354.9 10.7 %collective-permute-start = (f32[4,128,256]{2,1,0:T(8,128)}, f32[4,128,256]{2,1,0:T(8,128)S(1)}, u32[]{:S(2)}, u32[]{:S(2)}) collective-permute-start(f32[4,128,256]{2,1,0:T(8,128)} %convolution_add_fusion.5), channel_id=1, source_target_pairs={{0,4},{4,8},{8,12},{12,16},{16,20},{20,24},{24,28},{28,32},{32,36}... | collective-permute-start | bytes 1572872 | tf_op jit(solution)/shard_map/while/body/eval_jaxpr/ppermute | solution.py:15
  367.9 10.7 %collective-permute-start = (f32[4,128,256]{2,1,0:T(8,128)}, f32[4,128,256]{2,1,0:T(8,128)S(1)}, u32[]{:S(2)}, u32[]{:S(2)}) collective-permute-start(f32[4,128,256]{2,1,0:T(8,128)} %convolution_add_fusion.5), channel_id=1, source_target_pairs={{0,4},{4,8},{8,12},{12,16},{16,20},{20,24},{24,28},{28,32},{32,36}... | collective-permute-start | bytes 1572872 | tf_op jit(solution)/shard_map/while/body/eval_jaxpr/ppermute | solution.py:15
  380.9 10.7 %collective-permute-start = (f32[4,128,256]{2,1,0:T(8,128)}, f32[4,128,256]{2,1,0:T(8,128)S(1)}, u32[]{:S(2)}, u32[]{:S(2)}) collective-permute-start(f32[4,128,256]{2,1,0:T(8,128)} %convolution_add_fusion.5), channel_id=1, source_target_pairs={{0,4},{4,8},{8,12},{12,16},{16,20},{20,24},{24,28},{28,32},{32,36}... | collective-permute-start | bytes 1572872 | tf_op jit(solution)/shard_map/while/body/eval_jaxpr/ppermute | solution.py:15
  394.0 10.7 %collective-permute-start = (f32[4,128,256]{2,1,0:T(8,128)}, f32[4,128,256]{2,1,0:T(8,128)S(1)}, u32[]{:S(2)}, u32[]{:S(2)}) collective-permute-start(f32[4,128,256]{2,1,0:T(8,128)} %convolution_add_fusion.5), channel_id=1, source_target_pairs={{0,4},{4,8},{8,12},{12,16},{16,20},{20,24},{24,28},{28,32},{32,36}... | collective-permute-start | bytes 1572872 | tf_op jit(solution)/shard_map/while/body/eval_jaxpr/ppermute | solution.py:15
  407.0 10.7 %collective-permute-start = (f32[4,128,256]{2,1,0:T(8,128)}, f32[4,128,256]{2,1,0:T(8,128)S(1)}, u32[]{:S(2)}, u32[]{:S(2)}) collective-permute-start(f32[4,128,256]{2,1,0:T(8,128)} %convolution_add_fusion.5), channel_id=1, source_target_pairs={{0,4},{4,8},{8,12},{12,16},{16,20},{20,24},{24,28},{28,32},{32,36}... | collective-permute-start | bytes 1572872 | tf_op jit(solution)/shard_map/while/body/eval_jaxpr/ppermute | solution.py:15
  420.0 12.0 %collective-permute-start = (f32[4,128,256]{2,1,0:T(8,128)}, f32[4,128,256]{2,1,0:T(8,128)S(1)}, u32[]{:S(2)}, u32[]{:S(2)}) collective-permute-start(f32[4,128,256]{2,1,0:T(8,128)} %convolution_add_fusion.5), channel_id=1, source_target_pairs={{0,4},{4,8},{8,12},{12,16},{16,20},{20,24},{24,28},{28,32},{32,36}... | collective-permute-start | bytes 1572872 | tf_op jit(solution)/shard_map/while/body/eval_jaxpr/ppermute | solution.py:15
  434.4 12.8 %collective-permute-start = (f32[4,128,256]{2,1,0:T(8,128)}, f32[4,128,256]{2,1,0:T(8,128)S(1)}, u32[]{:S(2)}, u32[]{:S(2)}) collective-permute-start(f32[4,128,256]{2,1,0:T(8,128)} %convolution_add_fusion.5), channel_id=1, source_target_pairs={{0,4},{4,8},{8,12},{12,16},{16,20},{20,24},{24,28},{28,32},{32,36}... | collective-permute-start | bytes 1572872 | tf_op jit(solution)/shard_map/while/body/eval_jaxpr/ppermute | solution.py:15
  449.5 12.8 %collective-permute-start = (f32[4,128,256]{2,1,0:T(8,128)}, f32[4,128,256]{2,1,0:T(8,128)S(1)}, u32[]{:S(2)}, u32[]{:S(2)}) collective-permute-start(f32[4,128,256]{2,1,0:T(8,128)} %convolution_add_fusion.5), channel_id=1, source_target_pairs={{0,4},{4,8},{8,12},{12,16},{16,20},{20,24},{24,28},{28,32},{32,36}... | collective-permute-start | bytes 1572872 | tf_op jit(solution)/shard_map/while/body/eval_jaxpr/ppermute | solution.py:15
  464.6 12.8 %collective-permute-start = (f32[4,128,256]{2,1,0:T(8,128)}, f32[4,128,256]{2,1,0:T(8,128)S(1)}, u32[]{:S(2)}, u32[]{:S(2)}) collective-permute-start(f32[4,128,256]{2,1,0:T(8,128)} %convolution_add_fusion.5), channel_id=1, source_target_pairs={{0,4},{4,8},{8,12},{12,16},{16,20},{20,24},{24,28},{28,32},{32,36}... | collective-permute-start | bytes 1572872 | tf_op jit(solution)/shard_map/while/body/eval_jaxpr/ppermute | solution.py:15
  479.7 12.8 %collective-permute-start = (f32[4,128,256]{2,1,0:T(8,128)}, f32[4,128,256]{2,1,0:T(8,128)S(1)}, u32[]{:S(2)}, u32[]{:S(2)}) collective-permute-start(f32[4,128,256]{2,1,0:T(8,128)} %convolution_add_fusion.5), channel_id=1, source_target_pairs={{0,4},{4,8},{8,12},{12,16},{16,20},{20,24},{24,28},{28,32},{32,36}... | collective-permute-start | bytes 1572872 | tf_op jit(solution)/shard_map/while/body/eval_jaxpr/ppermute | solution.py:15
  494.9 12.8 %collective-permute-start = (f32[4,128,256]{2,1,0:T(8,128)}, f32[4,128,256]{2,1,0:T(8,128)S(1)}, u32[]{:S(2)}, u32[]{:S(2)}) collective-permute-start(f32[4,128,256]{2,1,0:T(8,128)} %convolution_add_fusion.5), channel_id=1, source_target_pairs={{0,4},{4,8},{8,12},{12,16},{16,20},{20,24},{24,28},{28,32},{32,36}... | collective-permute-start | bytes 1572872 | tf_op jit(solution)/shard_map/while/body/eval_jaxpr/ppermute | solution.py:15
  510.0 12.8 %collective-permute-start = (f32[4,128,256]{2,1,0:T(8,128)}, f32[4,128,256]{2,1,0:T(8,128)S(1)}, u32[]{:S(2)}, u32[]{:S(2)}) collective-permute-start(f32[4,128,256]{2,1,0:T(8,128)} %convolution_add_fusion.5), channel_id=1, source_target_pairs={{0,4},{4,8},{8,12},{12,16},{16,20},{20,24},{24,28},{28,32},{32,36}... | collective-permute-start | bytes 1572872 | tf_op jit(solution)/shard_map/while/body/eval_jaxpr/ppermute | solution.py:15
  525.1 12.8 %collective-permute-start = (f32[4,128,256]{2,1,0:T(8,128)}, f32[4,128,256]{2,1,0:T(8,128)S(1)}, u32[]{:S(2)}, u32[]{:S(2)}) collective-permute-start(f32[4,128,256]{2,1,0:T(8,128)} %convolution_add_fusion.5), channel_id=1, source_target_pairs={{0,4},{4,8},{8,12},{12,16},{16,20},{20,24},{24,28},{28,32},{32,36}... | collective-permute-start | bytes 1572872 | tf_op jit(solution)/shard_map/while/body/eval_jaxpr/ppermute | solution.py:15
  540.3 12.8 %collective-permute-start = (f32[4,128,256]{2,1,0:T(8,128)}, f32[4,128,256]{2,1,0:T(8,128)S(1)}, u32[]{:S(2)}, u32[]{:S(2)}) collective-permute-start(f32[4,128,256]{2,1,0:T(8,128)} %convolution_add_fusion.5), channel_id=1, source_target_pairs={{0,4},{4,8},{8,12},{12,16},{16,20},{20,24},{24,28},{28,32},{32,36}... | collective-permute-start | bytes 1572872 | tf_op jit(solution)/shard_map/while/body/eval_jaxpr/ppermute | solution.py:15
  555.4 12.8 %collective-permute-start = (f32[4,128,256]{2,1,0:T(8,128)}, f32[4,128,256]{2,1,0:T(8,128)S(1)}, u32[]{:S(2)}, u32[]{:S(2)}) collective-permute-start(f32[4,128,256]{2,1,0:T(8,128)} %convolution_add_fusion.5), channel_id=1, source_target_pairs={{0,4},{4,8},{8,12},{12,16},{16,20},{20,24},{24,28},{28,32},{32,36}... | collective-permute-start | bytes 1572872 | tf_op jit(solution)/shard_map/while/body/eval_jaxpr/ppermute | solution.py:15
  570.5 12.8 %collective-permute-start = (f32[4,128,256]{2,1,0:T(8,128)}, f32[4,128,256]{2,1,0:T(8,128)S(1)}, u32[]{:S(2)}, u32[]{:S(2)}) collective-permute-start(f32[4,128,256]{2,1,0:T(8,128)} %convolution_add_fusion.5), channel_id=1, source_target_pairs={{0,4},{4,8},{8,12},{12,16},{16,20},{20,24},{24,28},{28,32},{32,36}... | collective-permute-start | bytes 1572872 | tf_op jit(solution)/shard_map/while/body/eval_jaxpr/ppermute | solution.py:15
  585.7 12.8 %collective-permute-start = (f32[4,128,256]{2,1,0:T(8,128)}, f32[4,128,256]{2,1,0:T(8,128)S(1)}, u32[]{:S(2)}, u32[]{:S(2)}) collective-permute-start(f32[4,128,256]{2,1,0:T(8,128)} %convolution_add_fusion.5), channel_id=1, source_target_pairs={{0,4},{4,8},{8,12},{12,16},{16,20},{20,24},{24,28},{28,32},{32,36}... | collective-permute-start | bytes 1572872 | tf_op jit(solution)/shard_map/while/body/eval_jaxpr/ppermute | solution.py:15
  600.8 12.8 %collective-permute-start = (f32[4,128,256]{2,1,0:T(8,128)}, f32[4,128,256]{2,1,0:T(8,128)S(1)}, u32[]{:S(2)}, u32[]{:S(2)}) collective-permute-start(f32[4,128,256]{2,1,0:T(8,128)} %convolution_add_fusion.5), channel_id=1, source_target_pairs={{0,4},{4,8},{8,12},{12,16},{16,20},{20,24},{24,28},{28,32},{32,36}... | collective-permute-start | bytes 1572872 | tf_op jit(solution)/shard_map/while/body/eval_jaxpr/ppermute | solution.py:15
  637.6 91.4 %copy-start.16 = (s32[4]{0:T(128)S(1)}, s32[4]{0:T(128)}, u32[]{:S(2)}) copy-start(s32[4]{0:T(128)} %get-tuple-element.191) | copy-start | bytes 52
  637.6 214.9 %copy-start.12 = (f32[2048]{0:T(1024)S(1)}, f32[2048]{0:T(1024)}, u32[]{:S(2)}) copy-start(f32[2048]{0:T(1024)} %param.38) | copy-start | bytes 24580
  (25 other events, 53.3 us)
Sparse Core Ops, SparseCore 0:
  629.0 97.7 all-reduce.3
where the time goes:
time: 935 us; the launch traced here: 932 us
  waiting for transfers between devices  288 us (31%)
  blocking collectives  190 us (20%)
  starting transfers between devices  161 us (17%)
  matrix products  136 us (15%)
  other arithmetic  100 us (11%)
  local copies, waits for them, and re-layouts  40.7 us (4%)
  between operations  14.5 us (2%)
    ppermute x32, waiting for transfers between devices, from_behind(): lax.ppermute(value, axis, [(source, source + steps) for source in range(f...  199 us
    ppermute x32, starting transfers between devices, from_behind(): lax.ppermute(value, axis, [(source, source + steps) for source in range(f...  161 us
    psum x1, blocking collectives, body(): last_rows = lax.psum(picked.astype(jnp.bfloat16), 'seq').astype(jnp.float32)  123 us
    psum x1, waiting for transfers between devices, body(): summed = lax.psum(partial_out, 'tp')  89.2 us
    another operation x12, other arithmetic, block_step(): lax.linalg.triangular_solve(system_mat, right_side, left_side=True, lower...  81.6 us
    dot_general x31, matrix products, relay_turn(): jnp.einsum('hde,hef->hdf', lin_map, incoming, precision=HIGH) + offset_state  72.1 us
    pmax x1, blocking collectives, body(): max_logit = lax.pmax(jnp.max(logits, axis=1), ('seq', 'tp'))  67.2 us
  transfers between devices with their start and end apart: 33, of which 32 were waited for; matrix products, arithmetic and copies ran while one was open for 2% of the time, Pallas kernels for 0%

commit v1 on v0

--- a/solution.py
+++ b/solution.py
@@ -7,6 +7,7 @@
 BLOCK_LEN = 64
 EPS = 1e-06
 HIGH = lax.Precision.HIGHEST
+fix_array = lambda x0: jnp.sum(lax.all_gather(x0, axis_name="tp"), axis=0)
 
 
 def from_behind(value, axis, steps):
@@ -172,7 +173,7 @@
     col_start = lax.axis_index("tp") * share_cols
     last_tok = ends * BLOCK_LEN - 1
     picker = (last_tok[:, None] == positions[None, :]).astype(jnp.bfloat16)
-    summed = lax.psum(partial_out, "tp")
+    summed = fix_array(partial_out)
     hidden_full = (x_float + summed).astype(jnp.bfloat16)
     hidden = lax.dynamic_slice_in_dim(hidden_full, col_start, share_cols, 1)
     picked = jnp.dot(picker, hidden_full, preferred_element_type=jnp.float32)

time: 935 us -> 868 us (0.928)
  matrix products: 136 us -> 76.1 us
  local copies, waits for them, and re-layouts: 40.7 us -> 21.4 us
  waiting for transfers between devices: 288 us -> 303 us
    all_gather x0 -> x1, waiting for transfers between devices: none -> 114 us  [fix_array = lambda x0: jnp.sum(lax.all_gather(x0, axis_name='tp'), axis=0)]
    psum x1 -> x0, waiting for transfers between devices: 89.2 us -> none  [body(): summed = lax.psum(partial_out, 'tp')]
    dot_general x31, matrix products: 72.1 us -> 18.1 us  [relay_turn(): jnp.einsum('hde,hef->hdf', lin_map, incoming, precision=HIGH) + offset_state]
    ppermute x32, waiting for transfers between devices: 199 us -> 189 us  [from_behind(): lax.ppermute(value, axis, [(source, source + steps) for source in range(f...]
  transfers between devices with their start and end apart: 33 -> 33, of which waited for: 32 -> 32; matrix products, arithmetic and copies ran while one was open for 2% -> 1% of each run, Pallas kernels for 0% -> 0%
where the time goes in v1:
time: 868 us; the launch traced here: 867 us
  waiting for transfers between devices  303 us (35%)
  blocking collectives  190 us (22%)
  starting transfers between devices  167 us (19%)
  other arithmetic  93.4 us (11%)
  matrix products  76.1 us (9%)
  local copies, waits for them, and re-layouts  21.4 us (2%)
  between operations  14.6 us (2%)
    ppermute x32, waiting for transfers between devices, from_behind(): lax.ppermute(value, axis, [(source, source + steps) for source in range(f...  189 us
    ppermute x32, starting transfers between devices, from_behind(): lax.ppermute(value, axis, [(source, source + steps) for source in range(f...  167 us
    psum x1, blocking collectives, body(): last_rows = lax.psum(picked.astype(jnp.bfloat16), 'seq').astype(jnp.float32)  123 us
    all_gather x1, waiting for transfers between devices, fix_array = lambda x0: jnp.sum(lax.all_gather(x0, axis_name='tp'), axis=0)  114 us
    another operation x12, other arithmetic, block_step(): lax.linalg.triangular_solve(system_mat, right_side, left_side=True, lower...  78.7 us
    pmax x1, blocking collectives, body(): max_logit = lax.pmax(jnp.max(logits, axis=1), ('seq', 'tp'))  67.1 us
    dot_general x31, matrix products, relay_turn(): jnp.einsum('hde,hef->hdf', lin_map, incoming, precision=HIGH) + offset_state  18.1 us
  transfers between devices with their start and end apart: 33, of which 32 were waited for; matrix products, arithmetic and copies ran while one was open for 1% of the time, Pallas kernels for 0%

profile of v1, /device:TPU:1, one launch (start us, length us, event | category | flops | bytes accessed | tf_op | source)
XLA Modules:
  0.0 866.9 jit_solution(3189869595160729459)
XLA Ops:
  33.9 117.3 %while.24 = (s32[]{:T(128)}, f32[4,128,384]{2,1,0:T(8,128)S(1)}, f32[4,4,64,384]{3,2,0,1:T(8,128)}, f32[4,4,128,384]{3,2,1,0:T(8,128)}, f32[4,4,64]{2,1,0:T(4,12...) while((s32[]{:T(128)}, f32[4,128,384]{2,1,0:T(8,128)S(1)}, ...), condition=%wide.region_8.9_spmd, body=%wide.region_7.8_spmd.sunk | while | flops 656073024 | bytes 8813277 | solution.py:146
  34.4 19.7 %custom-call.8 = f32[4,1,64,64]{2,3,1,0:T(8,128)S(1)} custom-call(f32[4,1,64,64]{3,2,1,0:T(8,128)S(1)} %fusion.136), custom_call_target="InvertDiagBlocksLowerTriangular" | custom-call | tf_op jit(solution)/shard_map/while/body/eval_jaxpr/triangular_solve | solution.py:63
  63.8 19.7 %custom-call.8 = f32[4,1,64,64]{2,3,1,0:T(8,128)S(1)} custom-call(f32[4,1,64,64]{3,2,1,0:T(8,128)S(1)} %fusion.136), custom_call_target="InvertDiagBlocksLowerTriangular" | custom-call | tf_op jit(solution)/shard_map/while/body/eval_jaxpr/triangular_solve | solution.py:63
  93.1 19.7 %custom-call.8 = f32[4,1,64,64]{2,3,1,0:T(8,128)S(1)} custom-call(f32[4,1,64,64]{3,2,1,0:T(8,128)S(1)} %fusion.136), custom_call_target="InvertDiagBlocksLowerTriangular" | custom-call | tf_op jit(solution)/shard_map/while/body/eval_jaxpr/triangular_solve | solution.py:63
  122.4 19.7 %custom-call.8 = f32[4,1,64,64]{2,3,1,0:T(8,128)S(1)} custom-call(f32[4,1,64,64]{3,2,1,0:T(8,128)S(1)} %fusion.136), custom_call_target="InvertDiagBlocksLowerTriangular" | custom-call | tf_op jit(solution)/shard_map/while/body/eval_jaxpr/triangular_solve | solution.py:63
  151.3 369.9 %while.25 = (s32[]{:T(128)}, f32[4,128,256]{2,1,0:T(8,128)S(1)}, f32[4,128,128]{2,1,0:T(8,128)S(1)}, f32[4,128,256]{2,1,0:T(8,128)S(1)}, s32[]{:T(128)}) while((s32[]{:T(128)}, f32[4,128,256]{2,1,0:T(8,128)S(1)}, f32[4,128,128]{2,1,0:T(8,128)S(1)}, f32[4,128,256]{2,1,0:T(8,128)S(1)}, s32[]{:T(128)}) %tuple.76), condition=%wide.region_10.11_spmd, body=%wide.region_9.10_spmd.sunk | while | flops 201457664 | bytes 3932261 | solution.py:156
  153.9 6.1 collective-permute-done
  165.0 6.1 collective-permute-done
  176.1 6.1 collective-permute-done
  187.2 6.1 collective-permute-done
  198.3 6.1 collective-permute-done
  209.3 6.1 collective-permute-done
  220.4 6.1 collective-permute-done
  231.5 6.1 collective-permute-done
  242.6 6.1 collective-permute-done
  253.7 6.1 collective-permute-done
  264.8 6.1 collective-permute-done
  275.9 6.1 collective-permute-done
  287.0 6.1 collective-permute-done
  298.1 6.1 collective-permute-done
  309.2 6.1 collective-permute-done
  320.3 6.1 collective-permute-done
  331.4 6.1 collective-permute-done
  343.5 6.1 collective-permute-done
  350.2 6.5 collective-permute-start
  356.7 6.1 collective-permute-done
  363.4 6.5 collective-permute-start
  369.9 6.1 collective-permute-done
  376.6 6.5 collective-permute-start
  383.1 6.1 collective-permute-done
  389.8 6.5 collective-permute-start
  396.3 6.1 collective-permute-done
  403.0 6.5 collective-permute-start
  409.5 6.1 collective-permute-done
  416.2 6.5 collective-permute-start
  422.7 6.1 collective-permute-done
  429.4 6.5 collective-permute-start
  435.9 6.1 collective-permute-done
  442.6 6.5 collective-permute-start
  455.8 6.5 collective-permute-start
  469.0 6.5 collective-permute-start
  482.2 6.5 collective-permute-start
  495.4 6.5 collective-permute-start
  508.6 6.5 collective-permute-start
  527.6 7.6 fusion.47
  544.1 113.9 %all-gather.3.cloned.1.call-done = f32[1024,2048]{1,0:T(8,128)} async-done(((f32[256,2048]{1,0:T(8,128)}), f32[1024,2048]{1,0:T(8,128)}) %all-gather.3.cloned.1.call-update) | async-done | bytes 8388624 | tf_op jit(solution)/shard_map/all_gather | solution.py:10
  664.2 123.1 %psum.7 = bf16[4,2048]{1,0:T(4,128)(2,1)S(1)} all-reduce(bf16[4,2048]{1,0:T(4,128)(2,1)S(1)} %convolution_convert_fusion), channel_id=1, replica_groups=mesh['seq'=32,'tp'=4] {'seq'}, use_global_device_ids=true, to_apply=%region_13.14 | all-reduce | flops 8192 | bytes 32768 | tf_op jit(solution)/shard_map/psum | solution.py:180
  792.1 67.1 %pmax.7 = f32[4]{0:T(128)} all-reduce(f32[4]{0:T(128)S(1)} %convolution_reduce_fusion), channel_id=1, replica_groups=mesh['seq'=32,'tp'=4] {'seq','tp'}, use_global_device_ids=true, to_apply=%region_16.17 | all-reduce | flops 4 | bytes 32 | tf_op jit(solution)/shard_map/pmax | solution.py:183
  (242 shorter events, 223.9 us)
Async XLA Ops:
  7.2 5.7 copy-start
  7.2 650.8 %all-gather.3.cloned.1.call-start = ((), (), s32[]{:S(2)}) async-start(), calls=%async_computation | async-start | bytes 10485760 | tf_op jit(solution)/shard_map/all_gather | solution.py:10
  8.9 3.9 copy-start.3
  8.9 3.9 copy-start.18
  15.2 5.2 copy-start.14
  15.2 5.5 copy-start.11
  15.2 5.5 copy-start.12
  15.3 5.5 copy-start.9
  15.3 5.7 copy-start.19
  15.3 5.7 copy-start.4
  15.3 5.7 copy-start.16
  15.3 6.2 copy-start.13
  15.3 6.2 copy-start.17
  15.3 6.2 copy-start.20
  15.5 7.8 collective-permute-start.1
  151.9 8.1 collective-permute-start
  160.6 10.5 %collective-permute-start = (f32[4,128,256]{2,1,0:T(8,128)S(1)}, f32[4,128,256]{2,1,0:T(8,128)S(1)}, u32[]{:S(2)}, u32[]{:S(2)}) collective-permute-start(f32[4,128,256]{2,1,0:T(8,128)S(1)} %convolution_add_fusion.5), channel_id=1, source_target_pairs={{0,4},{4,8},{8,12},{12,16},{16,20},{20,24},{24,28},{28,32},{32,36}... | collective-permute-start | bytes 1572872 | tf_op jit(solution)/shard_map/while/body/eval_jaxpr/ppermute | solution.py:16
  171.7 10.5 %collective-permute-start = (f32[4,128,256]{2,1,0:T(8,128)S(1)}, f32[4,128,256]{2,1,0:T(8,128)S(1)}, u32[]{:S(2)}, u32[]{:S(2)}) collective-permute-start(f32[4,128,256]{2,1,0:T(8,128)S(1)} %convolution_add_fusion.5), channel_id=1, source_target_pairs={{0,4},{4,8},{8,12},{12,16},{16,20},{20,24},{24,28},{28,32},{32,36}... | collective-permute-start | bytes 1572872 | tf_op jit(solution)/shard_map/while/body/eval_jaxpr/ppermute | solution.py:16
  182.8 10.5 %collective-permute-start = (f32[4,128,256]{2,1,0:T(8,128)S(1)}, f32[4,128,256]{2,1,0:T(8,128)S(1)}, u32[]{:S(2)}, u32[]{:S(2)}) collective-permute-start(f32[4,128,256]{2,1,0:T(8,128)S(1)} %convolution_add_fusion.5), channel_id=1, source_target_pairs={{0,4},{4,8},{8,12},{12,16},{16,20},{20,24},{24,28},{28,32},{32,36}... | collective-permute-start | bytes 1572872 | tf_op jit(solution)/shard_map/while/body/eval_jaxpr/ppermute | solution.py:16
  193.8 10.5 %collective-permute-start = (f32[4,128,256]{2,1,0:T(8,128)S(1)}, f32[4,128,256]{2,1,0:T(8,128)S(1)}, u32[]{:S(2)}, u32[]{:S(2)}) collective-permute-start(f32[4,128,256]{2,1,0:T(8,128)S(1)} %convolution_add_fusion.5), channel_id=1, source_target_pairs={{0,4},{4,8},{8,12},{12,16},{16,20},{20,24},{24,28},{28,32},{32,36}... | collective-permute-start | bytes 1572872 | tf_op jit(solution)/shard_map/while/body/eval_jaxpr/ppermute | solution.py:16
  204.9 10.5 %collective-permute-start = (f32[4,128,256]{2,1,0:T(8,128)S(1)}, f32[4,128,256]{2,1,0:T(8,128)S(1)}, u32[]{:S(2)}, u32[]{:S(2)}) collective-permute-start(f32[4,128,256]{2,1,0:T(8,128)S(1)} %convolution_add_fusion.5), channel_id=1, source_target_pairs={{0,4},{4,8},{8,12},{12,16},{16,20},{20,24},{24,28},{28,32},{32,36}... | collective-permute-start | bytes 1572872 | tf_op jit(solution)/shard_map/while/body/eval_jaxpr/ppermute | solution.py:16
  216.0 10.5 %collective-permute-start = (f32[4,128,256]{2,1,0:T(8,128)S(1)}, f32[4,128,256]{2,1,0:T(8,128)S(1)}, u32[]{:S(2)}, u32[]{:S(2)}) collective-permute-start(f32[4,128,256]{2,1,0:T(8,128)S(1)} %convolution_add_fusion.5), channel_id=1, source_target_pairs={{0,4},{4,8},{8,12},{12,16},{16,20},{20,24},{24,28},{28,32},{32,36}... | collective-permute-start | bytes 1572872 | tf_op jit(solution)/shard_map/while/body/eval_jaxpr/ppermute | solution.py:16
  227.1 10.5 %collective-permute-start = (f32[4,128,256]{2,1,0:T(8,128)S(1)}, f32[4,128,256]{2,1,0:T(8,128)S(1)}, u32[]{:S(2)}, u32[]{:S(2)}) collective-permute-start(f32[4,128,256]{2,1,0:T(8,128)S(1)} %convolution_add_fusion.5), channel_id=1, source_target_pairs={{0,4},{4,8},{8,12},{12,16},{16,20},{20,24},{24,28},{28,32},{32,36}... | collective-permute-start | bytes 1572872 | tf_op jit(solution)/shard_map/while/body/eval_jaxpr/ppermute | solution.py:16
  238.2 10.5 %collective-permute-start = (f32[4,128,256]{2,1,0:T(8,128)S(1)}, f32[4,128,256]{2,1,0:T(8,128)S(1)}, u32[]{:S(2)}, u32[]{:S(2)}) collective-permute-start(f32[4,128,256]{2,1,0:T(8,128)S(1)} %convolution_add_fusion.5), channel_id=1, source_target_pairs={{0,4},{4,8},{8,12},{12,16},{16,20},{20,24},{24,28},{28,32},{32,36}... | collective-permute-start | bytes 1572872 | tf_op jit(solution)/shard_map/while/body/eval_jaxpr/ppermute | solution.py:16
  249.3 10.5 %collective-permute-start = (f32[4,128,256]{2,1,0:T(8,128)S(1)}, f32[4,128,256]{2,1,0:T(8,128)S(1)}, u32[]{:S(2)}, u32[]{:S(2)}) collective-permute-start(f32[4,128,256]{2,1,0:T(8,128)S(1)} %convolution_add_fusion.5), channel_id=1, source_target_pairs={{0,4},{4,8},{8,12},{12,16},{16,20},{20,24},{24,28},{28,32},{32,36}... | collective-permute-start | bytes 1572872 | tf_op jit(solution)/shard_map/while/body/eval_jaxpr/ppermute | solution.py:16
  260.4 10.5 %collective-permute-start = (f32[4,128,256]{2,1,0:T(8,128)S(1)}, f32[4,128,256]{2,1,0:T(8,128)S(1)}, u32[]{:S(2)}, u32[]{:S(2)}) collective-permute-start(f32[4,128,256]{2,1,0:T(8,128)S(1)} %convolution_add_fusion.5), channel_id=1, source_target_pairs={{0,4},{4,8},{8,12},{12,16},{16,20},{20,24},{24,28},{28,32},{32,36}... | collective-permute-start | bytes 1572872 | tf_op jit(solution)/shard_map/while/body/eval_jaxpr/ppermute | solution.py:16
  271.5 10.5 %collective-permute-start = (f32[4,128,256]{2,1,0:T(8,128)S(1)}, f32[4,128,256]{2,1,0:T(8,128)S(1)}, u32[]{:S(2)}, u32[]{:S(2)}) collective-permute-start(f32[4,128,256]{2,1,0:T(8,128)S(1)} %convolution_add_fusion.5), channel_id=1, source_target_pairs={{0,4},{4,8},{8,12},{12,16},{16,20},{20,24},{24,28},{28,32},{32,36}... | collective-permute-start | bytes 1572872 | tf_op jit(solution)/shard_map/while/body/eval_jaxpr/ppermute | solution.py:16
  282.6 10.5 %collective-permute-start = (f32[4,128,256]{2,1,0:T(8,128)S(1)}, f32[4,128,256]{2,1,0:T(8,128)S(1)}, u32[]{:S(2)}, u32[]{:S(2)}) collective-permute-start(f32[4,128,256]{2,1,0:T(8,128)S(1)} %convolution_add_fusion.5), channel_id=1, source_target_pairs={{0,4},{4,8},{8,12},{12,16},{16,20},{20,24},{24,28},{28,32},{32,36}... | collective-permute-start | bytes 1572872 | tf_op jit(solution)/shard_map/while/body/eval_jaxpr/ppermute | solution.py:16
  293.7 10.5 %collective-permute-start = (f32[4,128,256]{2,1,0:T(8,128)S(1)}, f32[4,128,256]{2,1,0:T(8,128)S(1)}, u32[]{:S(2)}, u32[]{:S(2)}) collective-permute-start(f32[4,128,256]{2,1,0:T(8,128)S(1)} %convolution_add_fusion.5), channel_id=1, source_target_pairs={{0,4},{4,8},{8,12},{12,16},{16,20},{20,24},{24,28},{28,32},{32,36}... | collective-permute-start | bytes 1572872 | tf_op jit(solution)/shard_map/while/body/eval_jaxpr/ppermute | solution.py:16
  304.8 10.5 %collective-permute-start = (f32[4,128,256]{2,1,0:T(8,128)S(1)}, f32[4,128,256]{2,1,0:T(8,128)S(1)}, u32[]{:S(2)}, u32[]{:S(2)}) collective-permute-start(f32[4,128,256]{2,1,0:T(8,128)S(1)} %convolution_add_fusion.5), channel_id=1, source_target_pairs={{0,4},{4,8},{8,12},{12,16},{16,20},{20,24},{24,28},{28,32},{32,36}... | collective-permute-start | bytes 1572872 | tf_op jit(solution)/shard_map/while/body/eval_jaxpr/ppermute | solution.py:16
  315.9 10.5 %collective-permute-start = (f32[4,128,256]{2,1,0:T(8,128)S(1)}, f32[4,128,256]{2,1,0:T(8,128)S(1)}, u32[]{:S(2)}, u32[]{:S(2)}) collective-permute-start(f32[4,128,256]{2,1,0:T(8,128)S(1)} %convolution_add_fusion.5), channel_id=1, source_target_pairs={{0,4},{4,8},{8,12},{12,16},{16,20},{20,24},{24,28},{28,32},{32,36}... | collective-permute-start | bytes 1572872 | tf_op jit(solution)/shard_map/while/body/eval_jaxpr/ppermute | solution.py:16
  327.0 10.5 %collective-permute-start = (f32[4,128,256]{2,1,0:T(8,128)S(1)}, f32[4,128,256]{2,1,0:T(8,128)S(1)}, u32[]{:S(2)}, u32[]{:S(2)}) collective-permute-start(f32[4,128,256]{2,1,0:T(8,128)S(1)} %convolution_add_fusion.5), channel_id=1, source_target_pairs={{0,4},{4,8},{8,12},{12,16},{16,20},{20,24},{24,28},{28,32},{32,36}... | collective-permute-start | bytes 1572872 | tf_op jit(solution)/shard_map/while/body/eval_jaxpr/ppermute | solution.py:16
  338.1 11.5 %collective-permute-start = (f32[4,128,256]{2,1,0:T(8,128)S(1)}, f32[4,128,256]{2,1,0:T(8,128)S(1)}, u32[]{:S(2)}, u32[]{:S(2)}) collective-permute-start(f32[4,128,256]{2,1,0:T(8,128)S(1)} %convolution_add_fusion.5), channel_id=1, source_target_pairs={{0,4},{4,8},{8,12},{12,16},{16,20},{20,24},{24,28},{28,32},{32,36}... | collective-permute-start | bytes 1572872 | tf_op jit(solution)/shard_map/while/body/eval_jaxpr/ppermute | solution.py:16
  350.2 12.6 %collective-permute-start = (f32[4,128,256]{2,1,0:T(8,128)S(1)}, f32[4,128,256]{2,1,0:T(8,128)S(1)}, u32[]{:S(2)}, u32[]{:S(2)}) collective-permute-start(f32[4,128,256]{2,1,0:T(8,128)S(1)} %convolution_add_fusion.5), channel_id=1, source_target_pairs={{0,4},{4,8},{8,12},{12,16},{16,20},{20,24},{24,28},{28,32},{32,36}... | collective-permute-start | bytes 1572872 | tf_op jit(solution)/shard_map/while/body/eval_jaxpr/ppermute | solution.py:16
  363.4 12.6 %collective-permute-start = (f32[4,128,256]{2,1,0:T(8,128)S(1)}, f32[4,128,256]{2,1,0:T(8,128)S(1)}, u32[]{:S(2)}, u32[]{:S(2)}) collective-permute-start(f32[4,128,256]{2,1,0:T(8,128)S(1)} %convolution_add_fusion.5), channel_id=1, source_target_pairs={{0,4},{4,8},{8,12},{12,16},{16,20},{20,24},{24,28},{28,32},{32,36}... | collective-permute-start | bytes 1572872 | tf_op jit(solution)/shard_map/while/body/eval_jaxpr/ppermute | solution.py:16
  376.6 12.6 %collective-permute-start = (f32[4,128,256]{2,1,0:T(8,128)S(1)}, f32[4,128,256]{2,1,0:T(8,128)S(1)}, u32[]{:S(2)}, u32[]{:S(2)}) collective-permute-start(f32[4,128,256]{2,1,0:T(8,128)S(1)} %convolution_add_fusion.5), channel_id=1, source_target_pairs={{0,4},{4,8},{8,12},{12,16},{16,20},{20,24},{24,28},{28,32},{32,36}... | collective-permute-start | bytes 1572872 | tf_op jit(solution)/shard_map/while/body/eval_jaxpr/ppermute | solution.py:16
  389.8 12.6 %collective-permute-start = (f32[4,128,256]{2,1,0:T(8,128)S(1)}, f32[4,128,256]{2,1,0:T(8,128)S(1)}, u32[]{:S(2)}, u32[]{:S(2)}) collective-permute-start(f32[4,128,256]{2,1,0:T(8,128)S(1)} %convolution_add_fusion.5), channel_id=1, source_target_pairs={{0,4},{4,8},{8,12},{12,16},{16,20},{20,24},{24,28},{28,32},{32,36}... | collective-permute-start | bytes 1572872 | tf_op jit(solution)/shard_map/while/body/eval_jaxpr/ppermute | solution.py:16
  403.0 12.6 %collective-permute-start = (f32[4,128,256]{2,1,0:T(8,128)S(1)}, f32[4,128,256]{2,1,0:T(8,128)S(1)}, u32[]{:S(2)}, u32[]{:S(2)}) collective-permute-start(f32[4,128,256]{2,1,0:T(8,128)S(1)} %convolution_add_fusion.5), channel_id=1, source_target_pairs={{0,4},{4,8},{8,12},{12,16},{16,20},{20,24},{24,28},{28,32},{32,36}... | collective-permute-start | bytes 1572872 | tf_op jit(solution)/shard_map/while/body/eval_jaxpr/ppermute | solution.py:16
  416.2 12.6 %collective-permute-start = (f32[4,128,256]{2,1,0:T(8,128)S(1)}, f32[4,128,256]{2,1,0:T(8,128)S(1)}, u32[]{:S(2)}, u32[]{:S(2)}) collective-permute-start(f32[4,128,256]{2,1,0:T(8,128)S(1)} %convolution_add_fusion.5), channel_id=1, source_target_pairs={{0,4},{4,8},{8,12},{12,16},{16,20},{20,24},{24,28},{28,32},{32,36}... | collective-permute-start | bytes 1572872 | tf_op jit(solution)/shard_map/while/body/eval_jaxpr/ppermute | solution.py:16
  429.4 12.6 %collective-permute-start = (f32[4,128,256]{2,1,0:T(8,128)S(1)}, f32[4,128,256]{2,1,0:T(8,128)S(1)}, u32[]{:S(2)}, u32[]{:S(2)}) collective-permute-start(f32[4,128,256]{2,1,0:T(8,128)S(1)} %convolution_add_fusion.5), channel_id=1, source_target_pairs={{0,4},{4,8},{8,12},{12,16},{16,20},{20,24},{24,28},{28,32},{32,36}... | collective-permute-start | bytes 1572872 | tf_op jit(solution)/shard_map/while/body/eval_jaxpr/ppermute | solution.py:16
  442.6 12.6 %collective-permute-start = (f32[4,128,256]{2,1,0:T(8,128)S(1)}, f32[4,128,256]{2,1,0:T(8,128)S(1)}, u32[]{:S(2)}, u32[]{:S(2)}) collective-permute-start(f32[4,128,256]{2,1,0:T(8,128)S(1)} %convolution_add_fusion.5), channel_id=1, source_target_pairs={{0,4},{4,8},{8,12},{12,16},{16,20},{20,24},{24,28},{28,32},{32,36}... | collective-permute-start | bytes 1572872 | tf_op jit(solution)/shard_map/while/body/eval_jaxpr/ppermute | solution.py:16
  455.8 12.6 %collective-permute-start = (f32[4,128,256]{2,1,0:T(8,128)S(1)}, f32[4,128,256]{2,1,0:T(8,128)S(1)}, u32[]{:S(2)}, u32[]{:S(2)}) collective-permute-start(f32[4,128,256]{2,1,0:T(8,128)S(1)} %convolution_add_fusion.5), channel_id=1, source_target_pairs={{0,4},{4,8},{8,12},{12,16},{16,20},{20,24},{24,28},{28,32},{32,36}... | collective-permute-start | bytes 1572872 | tf_op jit(solution)/shard_map/while/body/eval_jaxpr/ppermute | solution.py:16
  469.0 12.6 %collective-permute-start = (f32[4,128,256]{2,1,0:T(8,128)S(1)}, f32[4,128,256]{2,1,0:T(8,128)S(1)}, u32[]{:S(2)}, u32[]{:S(2)}) collective-permute-start(f32[4,128,256]{2,1,0:T(8,128)S(1)} %convolution_add_fusion.5), channel_id=1, source_target_pairs={{0,4},{4,8},{8,12},{12,16},{16,20},{20,24},{24,28},{28,32},{32,36}... | collective-permute-start | bytes 1572872 | tf_op jit(solution)/shard_map/while/body/eval_jaxpr/ppermute | solution.py:16
  482.2 12.6 %collective-permute-start = (f32[4,128,256]{2,1,0:T(8,128)S(1)}, f32[4,128,256]{2,1,0:T(8,128)S(1)}, u32[]{:S(2)}, u32[]{:S(2)}) collective-permute-start(f32[4,128,256]{2,1,0:T(8,128)S(1)} %convolution_add_fusion.5), channel_id=1, source_target_pairs={{0,4},{4,8},{8,12},{12,16},{16,20},{20,24},{24,28},{28,32},{32,36}... | collective-permute-start | bytes 1572872 | tf_op jit(solution)/shard_map/while/body/eval_jaxpr/ppermute | solution.py:16
  495.4 12.6 %collective-permute-start = (f32[4,128,256]{2,1,0:T(8,128)S(1)}, f32[4,128,256]{2,1,0:T(8,128)S(1)}, u32[]{:S(2)}, u32[]{:S(2)}) collective-permute-start(f32[4,128,256]{2,1,0:T(8,128)S(1)} %convolution_add_fusion.5), channel_id=1, source_target_pairs={{0,4},{4,8},{8,12},{12,16},{16,20},{20,24},{24,28},{28,32},{32,36}... | collective-permute-start | bytes 1572872 | tf_op jit(solution)/shard_map/while/body/eval_jaxpr/ppermute | solution.py:16
  508.6 12.6 %collective-permute-start = (f32[4,128,256]{2,1,0:T(8,128)S(1)}, f32[4,128,256]{2,1,0:T(8,128)S(1)}, u32[]{:S(2)}, u32[]{:S(2)}) collective-permute-start(f32[4,128,256]{2,1,0:T(8,128)S(1)} %convolution_add_fusion.5), channel_id=1, source_target_pairs={{0,4},{4,8},{8,12},{12,16},{16,20},{20,24},{24,28},{28,32},{32,36}... | collective-permute-start | bytes 1572872 | tf_op jit(solution)/shard_map/while/body/eval_jaxpr/ppermute | solution.py:16
  662.4 125.1 %copy-start.10 = (f32[2048]{0:T(1024)S(1)}, f32[2048]{0:T(1024)}, u32[]{:S(2)}) copy-start(f32[2048]{0:T(1024)} %param.38) | copy-start | bytes 24580
  787.5 72.5 %copy-start.1 = (bf16[2048,512]{1,0:T(8,128)(2,1)S(1)}, bf16[2048,512]{1,0:T(8,128)(2,1)}, u32[]{:S(2)}) copy-start(bf16[2048,512]{1,0:T(8,128)(2,1)} %param.26) | copy-start | bytes 6291460
  (7 other events, 13.3 us)
Sparse Core Ops, SparseCore 0:
  535.4 122.5 all-gather.2
